TPU v7x, 32 devices: a whole 2x2x4 slice. The times are simulated.
32 devices in a mesh: grp: 2 (over x), ctx: 4 (over z), wsh: 4 (over y, core).
Axes of the slice: x: 2, y: 2, z: 4, core: 2. Of those that a mesh axis runs over, the one named last changes fastest.
Arguments:
- inputs: bfloat16 [2, 4, 2048, 1024], P('grp', 'wsh', 'ctx'), may hold values from -6 to 6
- w_qkv: bfloat16 [1024, 3072], P('wsh'), may hold values from -0.1875 to 0.1875
- w_out: bfloat16 [1024, 1024], P('wsh'), may hold values from -0.1875 to 0.1875
- w_up: bfloat16 [1024, 4096], P('wsh'), may hold values from -0.1875 to 0.1875
- w_down: bfloat16 [4096, 1024], P('wsh'), may hold values from -0.09375 to 0.09375
- norm_gains: float32 [4, 1024], replicated, may hold values from 0.5 to 1.5
- norm_biases: float32 [4, 1024], replicated, may hold values from -2 to 2
- block_map: int32 [2, 4, 4, 2], P('grp', 'wsh', 'ctx'), may hold values from 0 to 1024, as said below
- out_grad: bfloat16 [2, 4, 2048, 1024], P('grp', 'wsh', 'ctx'), may hold values from -6 to 6
Outputs:
- output: bfloat16 [2, 4, 2048, 1024], P('grp', 'wsh', 'ctx')
- input_grad: float32 [2, 4, 2048, 1024], P('grp', 'wsh', 'ctx')
- grad_qkv: float32 [1024, 3072], P('wsh')
- grad_attn_out: float32 [1024, 1024], P('wsh')
- grad_up: float32 [1024, 4096], P('wsh')
- grad_down: float32 [4096, 1024], P('wsh')
- grad_gains: float32 [4, 1024], replicated
- grad_biases: float32 [4, 1024], replicated
Inputs may be any that keep to these rules, and one draw needn't show every extreme that they name: `block_map`: for each grp and wsh index the 4 context blocks are the 2 prompt blocks (sequence 0, first positions 0, 512, 1024 and so on) and one block of each continuation 1 to 4 // 2 (first position 1024), in an order drawn for each family.
All inputs are finite; a program needn't handle non-finite values.
Results may differ from a plain program's by a relative error of at most 0.017.
Values may be sent and summed in bfloat16 or wider, within the bound.
A program may use at most 384 MiB of HBM per device.

v0:
```python
import functools
import math

import jax
import jax.numpy as jnp
from jax import lax
from jax.experimental import pallas as pl
from jax.experimental.pallas import tpu as pltpu
from jax.sharding import PartitionSpec as P

D = 1024
HEADS = 16
DH = 64
BLK = 512
PAIRS = HEADS // 2
QT = 256

EPS = 1e-05
ALPHA = 32.0
NEG = -1e30
LOG2E = 1.4426950408889634
C2 = ALPHA * LOG2E
MESH = pl.DeviceIdType.MESH
QSCALE = 1.0 / (ALPHA * math.sqrt(DH))


def layer_norm(values, gain_row, bias_row):
    centre = values - jnp.mean(values, axis=-1, keepdims=True)
    spread = jnp.mean(centre * centre, axis=-1, keepdims=True)
    return centre * lax.rsqrt(spread + EPS) * gain_row + bias_row


def dot_dims(left_side, right_side, left_dim, right_dim):
    return lax.dot_general(
        left_side,
        right_side,
        (((left_dim,), (right_dim,)), ((), ())),
        preferred_element_type=jnp.float32,
    )


def contract_last(left_side, right_side):
    return dot_dims(left_side, right_side, 1, 1)


def contract_rows(left_side, right_side):
    return dot_dims(left_side, right_side, 0, 0)


def standard_rows(values):
    centre = values - jnp.mean(values, axis=-1, keepdims=True)
    scale = lax.rsqrt(jnp.mean(centre * centre, axis=-1, keepdims=True) + EPS)
    return centre * scale, scale


def row_back(upstream, hat, scale, gain):
    scaled = upstream * gain
    return scale * (
        scaled
        - jnp.mean(scaled, axis=-1, keepdims=True)
        - hat * jnp.mean(scaled * hat, axis=-1, keepdims=True)
    )


def column_sum(values):
    return jnp.sum(values, axis=0, keepdims=True)


def head_lanes(head, rows):
    lane = lax.broadcasted_iota(jnp.int32, (rows, 128), 1)
    return (lane >= DH) if head else (lane < DH)


def causal_tile():
    row = lax.broadcasted_iota(jnp.int32, (QT, QT), 0)
    col = lax.broadcasted_iota(jnp.int32, (QT, QT), 1)
    return col <= row


PIECE = 128
SPAN = 512
CHAIN = 64
HOP = 2
YLAG = 3
XLAG = 2
BLAG = 2
FF_TICKS = 13
TAIL_PACE = 3
GELU_A = 0.044715
GELU_C = math.sqrt(2.0 / math.pi)
PACE = 2
LAG = 2
GROUP = 4
AHEAD = 4


def remote(src, dst, send, recv, peer):
    return pltpu.make_async_remote_copy(
        src_ref=src, dst_ref=dst, send_sem=send, recv_sem=recv, device_id=peer, device_id_type=MESH
    )


def local_wait(ref, sem):
    pltpu.make_async_copy(ref, ref, sem).wait()


def aligned(start, size):
    return pl.ds(pl.multiple_of(start, size), size)


def softmax_block(q_ref, kv_ref, acc, top_ref, sum_ref, pair, base, own, visible):
    lanes = aligned(pair * 128, 128)
    value_lanes = aligned(D + pair * 128, 128)
    causal = causal_tile()
    first = head_lanes(0, QT)
    count = BLK // QT
    q_pair = q_ref[:, lanes]
    keys = kv_ref[pl.ds(base, BLK), lanes]
    values = kv_ref[pl.ds(base, BLK), value_lanes]
    if not own:
        old_top, old_sum, old_out = top_ref[pair], sum_ref[pair], acc[:, lanes]
        hide = jnp.where(visible, 0.0, 1e30)
    results = []
    work = [(tile, head) for tile in range(count) for head in range(2)]
    parts_of = {}
    for tile, head in work:
        q_tile = q_pair[tile * QT : (tile + 1) * QT]
        q_head = jnp.where(head_lanes(head, QT), q_tile, jnp.zeros_like(q_tile))
        span = (tile + 1) * QT if own else BLK
        parts_of[tile, head] = contract_last(q_head, keys[:span])
    top_of, expo_of, total_of = {}, {}, {}
    for tile, head in work:
        part = parts_of[tile, head]
        if own:
            diag = jnp.where(causal, part[:, tile * QT :], NEG)
            part = jnp.concatenate([part[:, : tile * QT], diag], axis=1) if tile else diag
        top = jnp.max(part, axis=-1, keepdims=True) * C2
        if own:
            shift = top
        else:
            top = jnp.maximum(
                jnp.where(visible, top, NEG), old_top[tile * QT : (tile + 1) * QT, head * DH : head * DH + 1]
            )
            shift = top + hide
        expo = jnp.exp2(part * C2 - shift)
        top_of[tile, head] = jnp.broadcast_to(top, (QT, 128))
        total_of[tile, head] = jnp.broadcast_to(jnp.sum(expo, axis=-1, keepdims=True), (QT, 128))
        expo_of[tile, head] = expo.astype(jnp.bfloat16)
    out_of = {}
    for tile, head in work:
        span = (tile + 1) * QT if own else BLK
        out_of[tile, head] = dot_dims(expo_of[tile, head], values[:span], 1, 0)
    for tile in range(count):
        rows = pl.ds(tile * QT, QT)
        new_top = jnp.where(first, top_of[tile, 0], top_of[tile, 1])
        new_sum = jnp.where(first, total_of[tile, 0], total_of[tile, 1])
        new_out = jnp.where(first, out_of[tile, 0], out_of[tile, 1])
        if not own:
            here = slice(tile * QT, (tile + 1) * QT)
            keep = jnp.exp2(old_top[here] - new_top)
            new_sum = new_sum + old_sum[here] * keep
            new_out = new_out + old_out[here] * keep
        top_ref[pair, rows, :] = new_top
        sum_ref[pair, rows, :] = new_sum
        acc[rows, lanes] = new_out


def forward_kernel(n_ctx, *refs):
    slots = n_ctx // 2
    (slot_ref, gain_ref, bias_ref, x_hbm, dy_hbm, w_qkv, w_out, w_up, w_down) = refs[:9]
    (a_out, q_out, kv_out, o_out, lse_out, full_qkv, full_out, full_up, full_down) = refs[9:18]
    (y_out, g_out, dz_out, f_out, u_out, hat1_out, hat2_out, rstd_out, norm_out) = refs[18:27]
    (x_own, left, right, a_all, q_all, kv_all, weight, acc, z_acc, norm_v, tops, sums, hop) = refs[27:40]
    (sem_in, sem_load, sem_store, sem_ff, sem_out, sem_a, sem_kv, side_s, side_r, grp_s, grp_r, cs_s, cs_r, cg_s, cg_r, own_s, own_r, left_s, left_r, right_s, right_r) = refs[40:]
    grp, ctx, wsh = lax.axis_index("grp"), lax.axis_index("ctx"), lax.axis_index("wsh")
    side, core = wsh // 2, wsh % 2
    core_peer = (grp, ctx, side * 2 + 1 - core)
    side_peer = (grp, ctx, (1 - side) * 2 + core)
    grp_peer = (1 - grp, ctx, wsh)
    next_ctx = (grp, lax.rem(ctx + 1, n_ctx), wsh)
    last_ctx = (grp, lax.rem(ctx + n_ctx - 1, n_ctx), wsh)

    load = pltpu.make_async_copy(x_hbm, x_own, sem_in.at[0])
    load.start()
    barrier = pltpu.get_barrier_semaphore()
    for peer in (core_peer, side_peer, grp_peer, next_ctx, last_ctx):
        pl.semaphore_signal(barrier, inc=1, device_id=peer, device_id_type=MESH)
    pl.semaphore_wait(barrier, 5)

    shards = (w_qkv, w_out, w_up, w_down)
    fulls = (weight, full_out, full_up, full_down)
    ranges, start = [], 0
    for shard in shards:
        across = shard.shape[1] // SPAN
        ranges.append((start, start + across * (shard.shape[0] // (2 * PIECE)), across))
        start = ranges[-1][1]
    pieces = start

    def by_range(index, act):
        for place, (low, high, across) in enumerate(ranges):

            @pl.when((index >= low) & (index < high))
            def _(place=place, low=low, across=across):
                act(place, (index - low) // across, aligned(((index - low) % across) * SPAN, SPAN))

    def rows_of(place, owner, half, group):
        shard_rows = shards[place].shape[0]
        return aligned(owner * shard_rows + half * (shard_rows // 2) + group * PIECE, PIECE)

    sides_owner = (1 - side) * 2 + core

    def send_piece(index, carry):
        def act(place, group, cols):
            remote(
                shards[place].at[rows_of(place, 0, grp, group), cols],
                fulls[place].at[rows_of(place, wsh, grp, group), cols],
                side_s.at[index],
                side_r.at[index],
                side_peer,
            ).start()

        by_range(index, act)
        return carry

    def own_copies():
        copies = []
        across = shards[0].shape[1] // SPAN
        for place in range(4):
            shard_rows = shards[place].shape[0]
            mine = aligned(wsh * shard_rows, shard_rows)
            steps = range(across) if place == 0 else [None]
            for step in steps:
                cols = slice(None) if step is None else pl.ds(step * SPAN, SPAN)
                number = len(copies)
                copies.append(
                    remote(
                        shards[place].at[:, cols],
                        fulls[place].at[mine, cols],
                        own_s.at[number],
                        own_r.at[number],
                        core_peer,
                    )
                )
        return copies

    for index in range(AHEAD):
        send_piece(index, 0)
    for copy in own_copies():
        copy.start()
    own_rows = aligned(wsh * w_qkv.shape[0], w_qkv.shape[0])
    own_weight = pltpu.make_async_copy(w_qkv, weight.at[own_rows, :], sem_in.at[1])
    own_weight.start()
    load.wait()

    bounces, start = [], 0
    for shard in shards[1:]:
        across = shard.shape[1] // SPAN
        bounces.append((start, start + across * (shard.shape[0] // (2 * PIECE)), across))
        start = bounces[-1][1]
    moves = start

    def bounce(index, loading):
        slot = lax.rem(index, 3)
        for place, (low, high, across) in enumerate(bounces):

            @pl.when((index >= low) & (index < high))
            def _(place=place + 1, low=low, across=across):
                group = (index - low) // across
                cols = aligned(((index - low) % across) * SPAN, SPAN)
                if loading:
                    here = shards[place].at[aligned(group * 2 * PIECE, 2 * PIECE), cols]
                    pltpu.make_async_copy(here, hop.at[slot], sem_load.at[slot]).start()
                else:
                    rows = aligned(wsh * shards[place].shape[0] + group * 2 * PIECE, 2 * PIECE)
                    local_wait(hop.at[slot], sem_load.at[slot])
                    pltpu.make_async_copy(
                        hop.at[slot], fulls[place].at[rows, cols], sem_store.at[slot]
                    ).start()

    own_slot = slot_ref[1] // BLK
    own_tag = jnp.where(slot_ref[0] == 0, own_slot, n_ctx)
    chain_chunks = slots * (BLK // CHAIN)

    def chain_step(stream, send, recv, number, is_first, is_last, target):
        slot = number // (BLK // CHAIN)
        spot = aligned((number % (BLK // CHAIN)) * CHAIN, CHAIN)
        mine = jnp.where(own_tag == slot, x_own[spot, :], jnp.zeros((CHAIN, D), jnp.bfloat16))
        here = stream.at[slot, spot]

        @pl.when(is_first)
        def _():
            stream[slot, spot, :] = mine

        @pl.when(jnp.logical_not(is_first))
        def _():
            remote(here, here, send.at[number], recv.at[number], target).wait_recv()
            stream[slot, spot, :] = stream[slot, spot, :] + mine

        @pl.when(jnp.logical_not(is_last))
        def _():
            remote(here, here, send.at[number], recv.at[number], target).start()

    def tick(step):
        @pl.when((step >= 1) & (step <= moves))
        def _():
            bounce(step - 1, False)

        @pl.when((step >= 3) & (step < moves))
        def _():
            local_wait(hop.at[lax.rem(step, 3)], sem_store.at[lax.rem(step, 3)])

        @pl.when(step < moves)
        def _():
            bounce(step, True)

        @pl.when(step + AHEAD < pieces)
        def _():
            send_piece(step + AHEAD, 0)

        number = step - HOP * ctx

        @pl.when((number >= 0) & (number < chain_chunks))
        def _():
            chain_step(left, left_s, left_r, number, ctx == 0, ctx == n_ctx - 1, next_ctx)

        back = step - HOP * (n_ctx - 1 - ctx)

        @pl.when((back >= 0) & (back < chain_chunks))
        def _():
            chain_step(right, right_s, right_r, back, ctx == n_ctx - 1, ctx == 0, last_ctx)

        @pl.when(step < pieces)
        def _():
            def act(place, group, cols):
                here = fulls[place].at[rows_of(place, sides_owner, grp, group), cols]
                remote(here, here, side_s.at[step], side_r.at[step], side_peer).wait_recv()
                remote(here, here, grp_s.at[step], grp_r.at[step], grp_peer).start()
                remote(here, here, cs_s.at[step], cs_r.at[step], core_peer).start()

            by_range(step, act)

        late = step - LAG

        @pl.when((late >= 0) & (late < pieces))
        def _():
            def act(place, group, cols):
                here = fulls[place].at[rows_of(place, sides_owner, 1 - grp, group), cols]
                remote(here, here, grp_s.at[late], grp_r.at[late], grp_peer).wait_recv()
                remote(here, here, cg_s.at[late], cg_r.at[late], core_peer).start()

            by_range(late, act)

    def ticks(first, last):
        lax.fori_loop(first, last, lambda index, carry: (tick(index), carry)[1], 0)

    def normalise(source, dest):
        gain, bias = gain_ref[0:1, :], bias_ref[0:1, :]

        def body(index, carry):
            rows = aligned(index * 128, 128)
            values = source(rows).astype(jnp.float32)
            a_all[aligned(dest + index * 128, 128), :] = layer_norm(values, gain, bias).astype(
                jnp.bfloat16
            )
            return carry

        lax.fori_loop(0, BLK // 128, body, 0)

    def piece_ready(index):
        here = fulls[0].at[pl.ds(0, PIECE), pl.ds(0, SPAN)]
        remote(here, here, cs_s.at[index], cs_r.at[index], core_peer).wait_recv()
        remote(here, here, cg_s.at[index], cg_r.at[index], core_peer).wait_recv()
        whole = fulls[0].at[pl.ds(0, 2 * PIECE), pl.ds(0, SPAN)]
        remote(whole, whole, own_s.at[index], own_r.at[index], core_peer).wait_recv()

    tick(0)
    normalise(lambda rows: x_own[rows, :], 0)
    ticks(1, LAG + 1)
    own_weight.wait()

    def project_q(index, carry):
        tick(index + LAG + 1)
        piece_ready(index)
        cols = aligned(index * SPAN, SPAN)
        q_all[:, cols] = (
            jnp.dot(a_all[pl.ds(0, BLK), :], weight[:, cols], preferred_element_type=jnp.float32) * QSCALE
        ).astype(jnp.bfloat16)
        return carry

    lax.fori_loop(0, D // SPAN, project_q, 0)
    head_ticks = LAG + 1 + D // SPAN

    def project_kv(index, base):
        cols = aligned(index * SPAN, SPAN)
        rows = aligned(base, BLK)
        kv_all[rows, cols] = jnp.dot(
            a_all[rows, :], weight[:, aligned(D + index * SPAN, SPAN)], preferred_element_type=jnp.float32
        ).astype(jnp.bfloat16)

    def own_kv(index, carry):
        tick(index + head_ticks)
        piece_ready(index + D // SPAN)
        project_kv(index, 0)
        return carry

    lax.fori_loop(0, 2 * D // SPAN, own_kv, 0)
    own_ticks = head_ticks + 2 * D // SPAN

    def send_block(index):
        rows = aligned(index * BLK, BLK)
        pltpu.make_async_copy(a_all.at[rows, :], a_out.at[rows, :], sem_a.at[index]).start()
        pltpu.make_async_copy(kv_all.at[rows, :], kv_out.at[rows, :], sem_kv.at[index]).start()

    outputs = [
        pltpu.make_async_copy(weight, full_qkv, sem_out.at[0]),
        pltpu.make_async_copy(q_all, q_out, sem_out.at[1]),
    ]
    for copy in outputs:
        copy.start()

    send_block(0)

    def own_attention(group, carry):
        ticks(own_ticks + 2 * group, own_ticks + 2 * group + 2)
        for member in range(GROUP):
            softmax_block(q_all, kv_all, acc, tops, sums, group * GROUP + member, 0, True, None)
        return carry

    groups = PAIRS // GROUP
    lax.fori_loop(0, groups, own_attention, 0)
    used = own_ticks + 2 * groups
    per_slot = 2 * D // SPAN + 2 * groups

    need = BLK // CHAIN + HOP * (n_ctx - 1)
    early = max(0, need - used)
    if early:
        lax.fori_loop(0, early, lambda index, carry: (tick(used + index), carry)[1], 0)

    def each_slot(slot, carry):
        base = pl.multiple_of((slot + 1) * BLK, BLK)
        visible = slot < own_slot
        begin = early + used + slot * per_slot

        def total(rows):
            joined = left[slot, rows, :] + right[slot, rows, :]
            return jnp.where(own_tag == slot, x_own[rows, :], joined)

        normalise(total, base)

        def slot_kv(index, inner):
            tick(begin + index)
            project_kv(index, base)
            return inner

        lax.fori_loop(0, 2 * D // SPAN, slot_kv, 0)

        send_block(slot + 1)

        def slot_attention(group, inner):
            start = begin + 2 * D // SPAN + 2 * group
            ticks(start, start + 2)
            for member in range(GROUP):
                softmax_block(
                    q_all, kv_all, acc, tops, sums, group * GROUP + member, base, False, visible
                )
            return inner

        lax.fori_loop(0, groups, slot_attention, 0)
        return carry

    lax.fori_loop(0, slots, each_slot, 0)
    done_ticks = early + used + slots * per_slot

    def finish(pair, carry):
        lanes = aligned(pair * 128, 128)
        x_own[:, lanes] = (acc[:, lanes] / sums[pair]).astype(jnp.bfloat16)
        tops[pair] = tops[pair] + jnp.log2(sums[pair])
        return carry

    lax.fori_loop(0, PAIRS, finish, 0)
    outputs += [
        pltpu.make_async_copy(x_own, o_out, sem_out.at[2]),
        pltpu.make_async_copy(tops, lse_out, sem_out.at[3]),
    ]
    for copy in outputs[2:]:
        copy.start()
    all_ticks = max(pieces + LAG, chain_chunks + HOP * (n_ctx - 1))
    if all_ticks > done_ticks:
        lax.fori_loop(done_ticks, all_ticks, lambda index, carry: (tick(index), carry)[1], 0)

    def drain(index, carry):
        here = fulls[0].at[pl.ds(0, PIECE), pl.ds(0, SPAN)]

        @pl.when(index >= ranges[0][1])
        def _():
            remote(here, here, cs_s.at[index], cs_r.at[index], core_peer).wait_recv()
            remote(here, here, cg_s.at[index], cg_r.at[index], core_peer).wait_recv()

        remote(here, here, side_s.at[index], side_r.at[index], side_peer).wait_send()
        remote(here, here, grp_s.at[index], grp_r.at[index], grp_peer).wait_send()
        remote(here, here, cs_s.at[index], cs_r.at[index], core_peer).wait_send()
        remote(here, here, cg_s.at[index], cg_r.at[index], core_peer).wait_send()
        return carry

    lax.fori_loop(0, pieces, drain, 0)
    copies = own_copies()
    for number, copy in enumerate(copies):
        copy.wait_send()
        if number >= len(copies) - 3:
            copy.wait_recv()
    for index in range(moves - 3, moves):
        local_wait(hop.at[index % 3], sem_store.at[index % 3])

    def drain_chain(index, carry):
        here = left.at[0, pl.ds(0, CHAIN)]

        @pl.when(ctx < n_ctx - 1)
        def _():
            remote(here, here, left_s.at[index], left_r.at[index], next_ctx).wait_send()

        @pl.when(ctx > 0)
        def _():
            remote(here, here, right_s.at[index], right_r.at[index], last_ctx).wait_send()

        return carry

    lax.fori_loop(0, chain_chunks, drain_chain, 0)
    for copy in outputs[:2]:
        copy.wait()
    shallow_tiles = full_up.shape[1] // SPAN

    def tile_loads(tile, parity):
        cols = aligned(tile * SPAN, SPAN)
        return (
            pltpu.make_async_copy(
                full_up.at[:, cols], weight.at[:, aligned(D + parity * SPAN, SPAN)], sem_ff.at[0, parity]
            ),
            pltpu.make_async_copy(full_down.at[cols, :], left.at[parity], sem_ff.at[1, parity]),
        )

    def tile_stores(tile, parity):
        cols = aligned(tile * SPAN, SPAN)
        return [
            pltpu.make_async_copy(
                kv_all.at[pl.ds(0, BLK), aligned(base + parity * SPAN, SPAN)],
                dest.at[:, cols],
                sem_ff.at[2 + place, parity],
            )
            for place, (base, dest) in enumerate(((0, u_out), (D, g_out)))
        ]

    out_load = pltpu.make_async_copy(full_out, weight.at[:, pl.ds(0, D)], sem_in.at[0])
    x_load = pltpu.make_async_copy(x_hbm, right.at[1], sem_in.at[1])
    for copy in (out_load, x_load) + tile_loads(0, 0):
        copy.start()

    def drain_blocks(index, carry):
        rows = aligned(index * BLK, BLK)
        local_wait(a_all.at[rows, :], sem_a.at[index])
        local_wait(kv_all.at[rows, :], sem_kv.at[index])
        return carry

    lax.fori_loop(0, slots + 1, drain_blocks, 0)
    out_load.wait()
    for half_cols in range(2):
        cols = pl.ds(half_cols * SPAN, SPAN)
        acc[:, cols] = jnp.dot(x_own[...], weight[:, cols], preferred_element_type=jnp.float32)
    x_load.wait()
    for copy in outputs[2:]:
        copy.wait()
    dy_load = pltpu.make_async_copy(dy_hbm, x_own, sem_in.at[0])
    dy_load.start()

    def inner_rows(step, carry):
        rows = aligned(step * CHAIN, CHAIN)
        hat, scale = standard_rows(acc[rows, :])
        a_all[rows, :] = hat.astype(jnp.bfloat16)
        sums[0, rows, :] = jnp.broadcast_to(scale, (CHAIN, 128))
        hidden = right[1, rows, :].astype(jnp.float32) + hat * gain_ref[1:2, :] + bias_ref[1:2, :]
        acc[rows, :] = hidden
        hat, scale = standard_rows(hidden)
        a_all[aligned(BLK + step * CHAIN, CHAIN), :] = hat.astype(jnp.bfloat16)
        sums[1, rows, :] = jnp.broadcast_to(scale, (CHAIN, 128))
        q_all[rows, :] = (hat * gain_ref[2:3, :] + bias_ref[2:3, :]).astype(jnp.bfloat16)
        return carry

    lax.fori_loop(0, BLK // CHAIN, inner_rows, 0)
    saves = [
        pltpu.make_async_copy(a_all.at[pl.ds(0, BLK), :], hat1_out, sem_out.at[0]),
        pltpu.make_async_copy(a_all.at[pl.ds(BLK, BLK), :], hat2_out, sem_out.at[1]),
        pltpu.make_async_copy(sums.at[pl.ds(0, 2)], rstd_out, sem_out.at[2]),
        pltpu.make_async_copy(q_all, f_out, sem_out.at[3]),
    ]
    for copy in saves:
        copy.start()

    def ff_tile(tile, carry):
        parity = tile % 2
        for copy in tile_loads(tile, parity):
            copy.wait()

        @pl.when(tile + 1 < shallow_tiles)
        def _():
            for copy in tile_loads(tile + 1, 1 - parity):
                copy.start()

        @pl.when(tile >= 2)
        def _():
            for copy in tile_stores(tile - 2, parity):
                copy.wait()

        upward = jnp.dot(
            q_all[...], weight[:, aligned(D + parity * SPAN, SPAN)], preferred_element_type=jnp.float32
        )
        kv_all[pl.ds(0, BLK), aligned(parity * SPAN, SPAN)] = upward.astype(jnp.bfloat16)
        active = (
            0.5 * upward * (1.0 + jnp.tanh(GELU_C * upward * (1.0 + GELU_A * upward * upward)))
        ).astype(jnp.bfloat16)
        kv_all[pl.ds(0, BLK), aligned(D + parity * SPAN, SPAN)] = active
        for copy in tile_stores(tile, parity):
            copy.start()
        fresh = jnp.dot(active, left[parity], preferred_element_type=jnp.float32)

        @pl.when(tile == 0)
        def _():
            z_acc[...] = fresh

        @pl.when(tile > 0)
        def _():
            z_acc[...] = z_acc[...] + fresh

        return carry

    lax.fori_loop(0, shallow_tiles, ff_tile, 0)
    dy_load.wait()

    def outer_rows(step, carry):
        gain_sum, bias_sum = carry
        rows = aligned(step * CHAIN, CHAIN)
        hat, scale = standard_rows(z_acc[rows, :])
        right[0, rows, :] = (acc[rows, :] + hat * gain_ref[3:4, :] + bias_ref[3:4, :]).astype(jnp.bfloat16)
        upstream = x_own[rows, :].astype(jnp.float32)
        a_all[aligned(2 * BLK + step * CHAIN, CHAIN), :] = row_back(
            upstream, hat, scale, gain_ref[3:4, :]
        ).astype(jnp.bfloat16)
        return gain_sum + column_sum(upstream * hat), bias_sum + column_sum(upstream)

    zero = jnp.zeros((1, D), jnp.float32)
    gain_sum, bias_sum = lax.fori_loop(0, BLK // CHAIN, outer_rows, (zero, zero))
    row = lax.broadcasted_iota(jnp.int32, (8, D), 0)
    norm_v[...] = jnp.where(row == 3, gain_sum, 0.0) + jnp.where(row == 7, bias_sum, 0.0)
    ends = [
        pltpu.make_async_copy(right.at[0], y_out, sem_in.at[0]),
        pltpu.make_async_copy(a_all.at[pl.ds(2 * BLK, BLK), :], dz_out, sem_in.at[1]),
        pltpu.make_async_copy(norm_v, norm_out, sem_in.at[2]),
    ]
    for copy in ends:
        copy.start()
    for tile in range(shallow_tiles - 2, shallow_tiles):
        for copy in tile_stores(tile, tile % 2):
            copy.wait()
    for copy in saves + ends:
        copy.wait()


def forward_part(n_ctx, tags, gains, biases, raw, dy, w_qkv, w_out, w_up, w_down):
    slots = n_ctx // 2
    every = (slots + 1) * BLK
    low, full = jnp.bfloat16, jnp.float32
    dma = pltpu.SemaphoreType.DMA
    hbm = pl.BlockSpec(memory_space=pl.ANY)
    vmem = pl.BlockSpec(memory_space=pltpu.VMEM)
    shards = (w_qkv, w_out, w_up, w_down)
    pieces = sum(w.shape[0] * w.shape[1] // (2 * PIECE * SPAN) for w in shards)
    own = w_qkv.shape[1] // SPAN + 3
    chain = slots * (BLK // CHAIN)
    shape = jax.ShapeDtypeStruct
    return pl.pallas_call(
        functools.partial(forward_kernel, n_ctx),
        out_shape=[
            shape((every, D), low),
            shape((BLK, D), low),
            shape((every, 2 * D), low),
            shape((BLK, D), low),
            shape((PAIRS, BLK, 128), full),
        ]
        + [shape((4 * w.shape[0], w.shape[1]), low) for w in shards]
        + [
            shape((BLK, D), low),
            shape((BLK, w_up.shape[1]), low),
            shape((BLK, D), low),
            shape((BLK, D), low),
            shape((BLK, w_up.shape[1]), low),
            shape((BLK, D), low),
            shape((BLK, D), low),
            shape((2, BLK, 128), full),
            shape((8, D), full),
        ],
        in_specs=[pl.BlockSpec(memory_space=pltpu.SMEM), vmem, vmem] + [hbm] * 6,
        out_specs=[hbm] * 18,
        scratch_shapes=[
            pltpu.VMEM((BLK, D), low),
            pltpu.VMEM((slots, BLK, D), low),
            pltpu.VMEM((slots, BLK, D), low),
            pltpu.VMEM((every, D), low),
            pltpu.VMEM((BLK, D), low),
            pltpu.VMEM((every, 2 * D), low),
            pltpu.VMEM((D, 3 * D), low),
            pltpu.VMEM((BLK, D), full),
            pltpu.VMEM((BLK, D), full),
            pltpu.VMEM((8, D), full),
            pltpu.VMEM((PAIRS, BLK, 128), full),
            pltpu.VMEM((PAIRS, BLK, 128), full),
            pltpu.VMEM((3, 2 * PIECE, SPAN), low),
            dma((3,)),
            dma((3,)),
            dma((3,)),
            dma((4, 2)),
            dma((4,)),
            dma((slots + 1,)),
            dma((slots + 1,)),
        ]
        + [dma((pieces,))] * 8
        + [dma((own,))] * 2
        + [dma((chain,))] * 4,
        compiler_params=pltpu.CompilerParams(
            collective_id=1, has_side_effects=True, vmem_limit_bytes=67043328
        ),
        cost_estimate=pl.CostEstimate(flops=20 << 30, bytes_accessed=64 << 20, transcendentals=1 << 24),
        name="gather_attend",
    )(tags, gains, biases, raw, dy, *shards)


TILE = 256
PAIRED = 2


def grad_block(q_ref, do_ref, o_ref, lse_ref, kv_ref, dq_acc, turned, pair, own, visible):
    lanes = aligned(pair * 128, 128)
    value_lanes = aligned(D + pair * 128, 128)
    size = QT if own else BLK
    count = BLK // size
    q_pair, do_pair, lse_pair = q_ref[:, lanes], do_ref[:, lanes], lse_ref[pair]
    prod = do_pair.astype(jnp.float32) * o_ref[:, lanes].astype(jnp.float32)
    keys, values = kv_ref[:, lanes], kv_ref[:, value_lanes]
    q_turned, do_turned = q_pair.T, do_pair.T
    old_dq = dq_acc[:, lanes]
    causal = causal_tile()
    hide = 0.0 if own else jnp.where(visible, 0.0, 1e30)
    lanes_of = [head_lanes(head, size) for head in range(2)]
    work = [(tile, head) for tile in range(count) for head in range(2)]
    score, dprob, dlogit, prob_low = {}, {}, {}, {}
    for tile, head in work:
        rows = slice(tile * size, (tile + 1) * size)
        span = (tile + 1) * size if own else BLK
        zero = jnp.zeros((size, 128), jnp.bfloat16)
        score[tile, head] = contract_last(jnp.where(lanes_of[head], q_pair[rows], zero), keys[:span])
        dprob[tile, head] = contract_last(jnp.where(lanes_of[head], do_pair[rows], zero), values[:span])
    for tile, head in work:
        rows = slice(tile * size, (tile + 1) * size)
        delta = jnp.sum(jnp.where(lanes_of[head], prod[rows], 0.0), axis=-1, keepdims=True)
        shift = lse_pair[rows, head * DH : head * DH + 1] + hide
        prob = jnp.exp2(score[tile, head] * C2 - shift)
        if own:
            diag = jnp.where(causal, prob[:, tile * size :], 0.0)
            prob = jnp.concatenate([prob[:, : tile * size], diag], axis=1) if tile else diag
        dlogit[tile, head] = (prob * (dprob[tile, head] - delta)).astype(jnp.bfloat16)
        prob_low[tile, head] = prob.astype(jnp.bfloat16)
    for tile in range(count):
        rows = slice(tile * size, (tile + 1) * size)
        span = (tile + 1) * size if own else BLK
        parts = [dot_dims(dlogit[tile, head], keys[:span], 1, 0) for head in range(2)]
        dq_acc[pl.ds(tile * size, size), lanes] = old_dq[rows] + jnp.where(lanes_of[0], parts[0], parts[1])
    for head in range(2):
        for offset, left_side, right_side, scale in (
            (0, q_turned, dlogit, ALPHA),
            (D, do_turned, prob_low, 1.0),
        ):
            spot = aligned(offset + pair * 128 + head * DH, DH)
            left_head = left_side[head * DH : (head + 1) * DH]
            terms = [
                dot_dims(left_head[:, tile * size : (tile + 1) * size], right_side[tile, head], 1, 0)
                for tile in range(count)
            ]
            for tile in range(count):
                cols = slice(tile * size, (tile + 1) * size)
                total = functools.reduce(
                    jnp.add, [terms[other][:, cols] for other in range(tile, count)]
                ) if own else terms[0]
                turned[spot, cols if own else slice(None)] = (total * scale).astype(jnp.bfloat16)


def backward_kernel(n_ctx, widths, *refs):
    slots = n_ctx // 2
    levels = n_ctx.bit_length() - 1
    depth = 16 if n_ctx == 4 else 10
    shallow = slots <= 2
    (slot_ref, gain_ref, bias_ref, norm_ref, x_hbm, q_hbm, kv_hbm, a_hbm, o_hbm, lse_hbm, w_hbm) = refs[:11]
    (w_out, w_up, w_down, g_hbm, dz_hbm, f_hbm, u_hbm, hat1_hbm, hat2_hbm, rstd_hbm, dy_hbm) = refs[11:22]
    outs = refs[22:26]
    grad_out, norm_out, dh_hbm, du_hbm, datt_hbm = refs[26:31]
    scratch = list(refs[31:])
    own_slot = slot_ref[1] // BLK

    def take(count):
        taken = scratch[:count]
        del scratch[:count]
        return taken

    q_v, o_v, do_v, lse_v, weight, kv_b, a_b, dq_acc, turned, gkv, term, own_part, left, right, norm_v, norm_in, gain_sum, bias_sum = take(18)
    r1, r2, r3, fin, made = take(5)
    lhs, rhs = take(2)
    zbufs = take(levels)
    sem_in, sem_blk, sem_rhs, sem_lhs, sem_ff, sem_out, sem_res = take(7)
    send1, recv1, send2, recv2, send3, recv3, send6, recv6 = take(8)
    rs_send, rs_recv, ag_send, ag_recv = take(levels), take(levels), take(levels), take(levels)
    left_s, left_r, right_s, right_r, norm_s, norm_r = take(6)
    grp, ctx, wsh = lax.axis_index("grp"), lax.axis_index("ctx"), lax.axis_index("wsh")
    side, core = wsh // 2, wsh % 2
    core_peer = (grp, ctx, side * 2 + 1 - core)
    side_peer = (grp, ctx, (1 - side) * 2 + core)
    grp_peer = (1 - grp, ctx, wsh)
    next_ctx = (grp, lax.rem(ctx + 1, n_ctx), wsh)
    last_ctx = (grp, lax.rem(ctx + n_ctx - 1, n_ctx), wsh)
    bits = [(ctx // (1 << level)) % 2 for level in range(levels)]
    level_peers = [(grp, ctx + (1 - 2 * bits[level]) * (1 << level), wsh) for level in range(levels)]

    def block_copies(index):
        rows = aligned(lax.rem(index, slots + 1) * BLK, BLK)
        slot = lax.rem(index, kv_b.shape[0])
        a_slot = index - 1 if shallow else 0
        return (
            pltpu.make_async_copy(kv_hbm.at[rows, :], kv_b.at[slot], sem_blk.at[0, slot]),
            pltpu.make_async_copy(a_hbm.at[rows, :], a_b.at[a_slot], sem_blk.at[1, slot]),
        )

    barrier = pltpu.get_barrier_semaphore()
    peers = [core_peer, side_peer, grp_peer, next_ctx, last_ctx] + level_peers
    for peer in peers:
        pl.semaphore_signal(barrier, inc=1, device_id=peer, device_id_type=MESH)
    pl.semaphore_wait(barrier, len(peers))

    half = TILE // 2
    ranges, first = [], 0
    for rows, cols in widths:
        across = cols // TILE
        ranges.append((first, first + (rows // TILE) * across, across))
        first = ranges[-1][1]
    chunks = first

    def by_range(index, act):
        for place, (low, high, across) in enumerate(ranges):

            @pl.when((index >= low) & (index < high))
            def _(place=place, low=low, across=across):
                number = index - low
                act(place, (aligned((number // across) * TILE, TILE), aligned((number % across) * TILE, TILE)))

    def region(level, flip):
        row, rows, col, cols = 0, half, 0, TILE
        for place in range(level):
            bit = 1 - bits[place] if (flip and place == level - 1) else bits[place]
            if rows > 16:
                rows = rows // 2
                row = row + bit * rows
            else:
                cols = cols // 2
                col = col + bit * cols
        return row, rows, col, cols

    def spot(level, flip=False, base=0):
        row, rows, col, cols = region(level, flip)
        return aligned(base + row, rows), aligned(col, cols)

    last_low = ranges[-1][0]
    dq_low = o_v
    set_of = [(0, number) for number in range(widths[0][0] // TILE)] + [(1, 0), (2, 0)]
    set_first = [number * ranges[0][2] for number in range(widths[0][0] // TILE)]
    set_first += [ranges[1][0], ranges[2][0]]
    left_of, right_of = (g_hbm, f_hbm, o_hbm), (dz_hbm, du_hbm, datt_hbm)

    def set_copies(number):
        place, group = set_of[number]
        stride = left_of[place].shape[1] // 4
        return [
            pltpu.make_async_copy(
                left_of[place].at[:, pl.ds(owner * stride + group * TILE, TILE)],
                lhs.at[number % 2, owner],
                sem_lhs.at[number % 2, owner],
            )
            for owner in range(4)
        ]

    def step_fetch(index):
        near = lax.rem(index, 4)

        def act(place, span):
            if place < 3:
                pltpu.make_async_copy(
                    right_of[place].at[:, span[1]], rhs.at[near], sem_rhs.at[near]
                ).start()

        by_range(index, act)

    def step_make(index, kinds):
        slot = lax.rem(index, depth)
        near = lax.rem(index, 4)

        def low_piece():
            local_wait(rhs.at[near], sem_rhs.at[near])
            parity = jnp.int32(0)
            for number, low in enumerate(set_first):
                parity = jnp.where(index >= low, number % 2, parity)

                @pl.when(index == low)
                def _(number=number):
                    for copy in set_copies(number):
                        copy.wait()
                    if number + 1 < len(set_first):
                        for copy in set_copies(number + 1):
                            copy.start()

            right_side = rhs[near]
            for owner in range(4):
                made[near, owner // 2, owner % 2] = dot_dims(
                    lhs[parity, owner], right_side, 0, 0
                ).astype(jnp.bfloat16)

        def high_piece():
            number = index - last_low
            if not shallow:
                made[near] = term[:, :, :, aligned(number * TILE, TILE)]
                return

            @pl.when(number < D // TILE)
            def _():
                right_side = dq_low[:, aligned(number * TILE, TILE)]
                for owner in range(4):
                    made[near, owner // 2, owner % 2] = dot_dims(
                        a_b[slots, :, pl.ds(owner * TILE, TILE)], right_side, 0, 0
                    ).astype(jnp.bfloat16)

            @pl.when(number >= D // TILE)
            def _():
                cols = aligned((number - D // TILE) * TILE, TILE)
                for owner in range(4):
                    total = functools.reduce(
                        jnp.add,
                        [
                            dot_dims(a_b[block, :, pl.ds(owner * TILE, TILE)], turned[block, cols, :], 0, 1)
                            for block in range(slots + 1)
                        ],
                    )
                    made[near, owner // 2, owner % 2] = total.astype(jnp.bfloat16)

        if kinds == "low":
            low_piece()
        elif kinds == "high":
            high_piece()
        else:
            pl.when(index < last_low)(low_piece)
            pl.when(index >= last_low)(high_piece)
        remote(
            made.at[near, :, 1 - core], r1.at[slot], send1.at[slot], recv1.at[slot], core_peer
        ).start()

    def finished(move):
        move.wait_send()
        move.wait_recv()

    def step_core(index):
        slot, near = lax.rem(index, depth), lax.rem(index, 4)
        finished(remote(r1.at[slot], r1.at[slot], send1.at[slot], recv1.at[slot], core_peer))
        r1[slot] = r1[slot] + made[near, :, core]
        remote(r1.at[slot, 1 - side], r2.at[slot], send2.at[slot], recv2.at[slot], side_peer).start()

    keep_half = aligned(grp * half, half)
    give_half = aligned((1 - grp) * half, half)

    def step_side(index):
        slot = lax.rem(index, depth)
        finished(remote(r1.at[slot, 1 - side], r2.at[slot], send2.at[slot], recv2.at[slot], side_peer))
        r2[slot] = r2[slot] + r1[slot, side]
        remote(r2.at[slot, give_half], r3.at[slot], send3.at[slot], recv3.at[slot], grp_peer).start()

    fold = n_ctx == 4
    if fold:
        outer = bits[0] == bits[1]
        inner = bits[0] != bits[1]
        mate, middle = level_peers[0], (grp, 3 - ctx, wsh)
        quarter = half // 2
        mine, other = aligned(bits[1] * quarter, quarter), aligned((1 - bits[1]) * quarter, quarter)
        fin_mine = aligned(grp * half + bits[1] * quarter, quarter)
        fin_other = aligned(grp * half + (1 - bits[1]) * quarter, quarter)

        def up_copy(slot):
            return remote(r3.at[slot], zbufs[0].at[slot], rs_send[0].at[slot], rs_recv[0].at[slot], mate)

        def cross_copy(slot):
            return remote(
                r3.at[slot, other], zbufs[1].at[slot], rs_send[1].at[slot], rs_recv[1].at[slot], middle
            )

        def share_copy(slot, rows):
            here = fin.at[slot, rows]
            return remote(here, here, ag_send[1].at[slot], ag_recv[1].at[slot], middle)

        def down_copy(slot):
            here = fin.at[slot, keep_half]
            return remote(here, here, ag_send[0].at[slot], ag_recv[0].at[slot], mate)

        def step_up(index):
            slot = lax.rem(index, depth)

            @pl.when(outer)
            def _():
                up_copy(slot).wait_send()

            @pl.when(inner)
            def _():
                up_copy(slot).wait_recv()
                r3[slot] = r3[slot] + zbufs[0][slot]
                cross_copy(slot).start()

        def step_cross(index):
            slot = lax.rem(index, depth)

            @pl.when(inner)
            def _():
                finished(cross_copy(slot))
                fin[slot, fin_mine] = r3[slot, mine] + zbufs[1][slot]
                share_copy(slot, fin_mine).start()

        def step_share(index):
            slot = lax.rem(index, depth)

            @pl.when(inner)
            def _():
                finished(share_copy(slot, fin_other))
                down_copy(slot).start()

        def step_down(index):
            slot = lax.rem(index, depth)

            @pl.when(inner)
            def _():
                down_copy(slot).wait_send()

            @pl.when(outer)
            def _():
                down_copy(slot).wait_recv()

            back_copy(slot, keep_half).start()

    def rs_copy(level, slot):
        rows, cols = spot(level + 1, True)
        return remote(
            r3.at[slot, rows, cols], zbufs[level].at[slot], rs_send[level].at[slot], rs_recv[level].at[slot], level_peers[level]
        )

    def ag_copy(level, slot, flip=False):
        rows, cols = spot(level + 1, flip, grp * half)
        here = fin.at[slot, rows, cols]
        return remote(here, here, ag_send[level].at[slot], ag_recv[level].at[slot], level_peers[level])

    def back_copy(slot, rows):
        here = fin.at[slot, rows]
        return remote(here, here, send6.at[slot], recv6.at[slot], grp_peer)

    def step_grp(index):
        slot = lax.rem(index, depth)
        finished(remote(r2.at[slot, give_half], r3.at[slot], send3.at[slot], recv3.at[slot], grp_peer))
        r3[slot] = r3[slot] + r2[slot, keep_half]
        if fold:

            @pl.when(outer)
            def _():
                up_copy(slot).start()
        else:
            rs_copy(0, slot).start()

    def step_scatter(level):
        def act(index):
            slot = lax.rem(index, depth)
            finished(rs_copy(level, slot))
            rows, cols = spot(level + 1)
            total = r3[slot, rows, cols] + zbufs[level][slot]
            if level + 1 < levels:
                r3[slot, rows, cols] = total
                rs_copy(level + 1, slot).start()
            else:
                rows, cols = spot(level + 1, False, grp * half)
                fin[slot, rows, cols] = total
                ag_copy(level, slot).start()

        return act

    def step_gather(level):
        def act(index):
            slot = lax.rem(index, depth)
            finished(ag_copy(level, slot, True))
            if level:
                ag_copy(level - 1, slot).start()
            else:
                back_copy(slot, keep_half).start()

        return act

    def out_wait(index):
        slot = lax.rem(index, depth)
        local_wait(fin.at[slot], sem_out.at[slot])

    def step_out(index):
        slot = lax.rem(index, depth)
        finished(back_copy(slot, give_half))

        def act(place, span):
            pltpu.make_async_copy(fin.at[slot], outs[place].at[span[0], span[1]], sem_out.at[slot]).start()

        by_range(index, act)

    z_lag = 2 if fold else 1
    order = [(YLAG, step_side), (XLAG, step_grp)]
    if fold:
        order += [(z_lag, act) for act in (step_up, step_cross, step_share, step_down)]
    else:
        order += [(z_lag, step_scatter(level)) for level in range(levels)]
        order += [(z_lag, step_gather(level)) for level in reversed(range(levels))]
    order += [(BLAG, step_out), (2, out_wait)]
    stages = [(0, step_core)]
    for lag, act in order:
        stages.append((stages[-1][0] + lag, act))
    all_ticks = chunks + stages[-1][0]

    per_slot = BLK // CHAIN
    chain_chunks = slots * per_slot

    def chain_step(stream, send, recv, number, is_first, is_last, target):
        slot = number // per_slot
        rows = aligned((number % per_slot) * CHAIN, CHAIN)
        here = stream.at[slot, rows]

        @pl.when(is_first)
        def _():
            stream[slot, rows, :] = own_part[slot, rows, :]

        @pl.when(jnp.logical_not(is_first))
        def _():
            remote(here, here, send.at[number], recv.at[number], target).wait_recv()
            stream[slot, rows, :] = stream[slot, rows, :] + own_part[slot, rows, :]

        @pl.when(jnp.logical_not(is_last))
        def _():
            remote(here, here, send.at[number], recv.at[number], target).start()

    def chain_tick(step):
        number = step - ctx

        @pl.when((number >= 0) & (number < chain_chunks))
        def _():
            chain_step(left, left_s, left_r, number, ctx == 0, ctx == n_ctx - 1, next_ctx)

        back = step - (n_ctx - 1 - ctx)

        @pl.when((back >= 0) & (back < chain_chunks))
        def _():
            chain_step(right, right_s, right_r, back, ctx == n_ctx - 1, ctx == 0, last_ctx)

    groups = PAIRS // PAIRED
    group_ticks = groups if shallow else 0
    block_ticks = group_ticks + 2
    chain_first = FF_TICKS + block_ticks
    paced = max(0, -(-(chunks - chain_first) // PACE))
    late_first = max(chunks, chain_first)
    late_beats = max(0, chain_chunks + n_ctx - 1 - paced)
    chain_ticks = late_first + TAIL_PACE * max(0, late_beats - 1) + 1

    def tick(step, kinds):
        kinds = kinds if shallow or kinds == "none" else "both"
        if kinds in ("low", "both"):

            @pl.when(step + 3 < chunks)
            def _():
                step_fetch(step + 3)

        if kinds != "none":

            @pl.when(step + 2 < chunks)
            def _():
                step_make(step + 2, kinds)

        for lag, act in stages:
            index = step - lag

            @pl.when((index >= 0) & (index < chunks))
            def _(act=act, index=index):
                act(index)

        beat = step - chain_first

        @pl.when((beat >= 0) & (step < chunks) & (beat % PACE == 0))
        def _():
            chain_tick(beat // PACE)

        late = step - late_first

        @pl.when((late >= 0) & (late % TAIL_PACE == 0))
        def _():
            chain_tick(paced + late // TAIL_PACE)


    for index in range(3):
        step_fetch(jnp.int32(index))
    for copy in set_copies(0):
        copy.start()

    hidden_tiles = u_hbm.shape[1] // SPAN
    datt_v, dz_v, dy_v, hat1_v, hat2_v = own_part.at[0], do_v, left.at[1], right.at[0], right.at[1]

    def tile_copies(tile, parity):
        cols = aligned(tile * SPAN, SPAN)
        return (
            pltpu.make_async_copy(w_down.at[cols, :], own_part.at[parity], sem_ff.at[0, parity]),
            pltpu.make_async_copy(
                w_up.at[:, cols], turned.at[0, aligned(parity * D, D), :], sem_ff.at[1, parity]
            ),
            pltpu.make_async_copy(
                u_hbm.at[:, cols], left.at[0, :, aligned(parity * SPAN, SPAN)], sem_ff.at[2, parity]
            ),
        )

    def du_store(tile, parity):
        return pltpu.make_async_copy(
            kv_b.at[0, :, aligned(parity * SPAN, SPAN)],
            du_hbm.at[:, aligned(tile * SPAN, SPAN)],
            sem_ff.at[3, parity],
        )

    dz_load = pltpu.make_async_copy(dz_hbm, dz_v, sem_in.at[0])
    dz_load.start()
    for copy in tile_copies(0, 0):
        copy.start()
    wide_loads = [
        pltpu.make_async_copy(source, dest, sem_in.at[place + 1])
        for place, (source, dest) in enumerate(
            (
                (dy_hbm, dy_v),
                (hat1_hbm, hat1_v),
                (hat2_hbm, hat2_v),
                (rstd_hbm, lse_v.at[pl.ds(0, 2)]),
                (q_hbm, q_v),
                (o_hbm, o_v),
                (w_hbm, weight),
            )
        )
    ]
    out_loads = [
        pltpu.make_async_copy(
            w_out.at[pl.ds(place * TILE, TILE), :],
            term.at[place // 2, place % 2, :, pl.ds(0, D)],
            sem_in.at[8 + place],
        )
        for place in range(4)
    ]
    lax.fori_loop(0, 2, lambda index, carry: (step_make(index, "low"), carry)[1], 0)
    dz_load.wait()

    def ff_tile(tile, carry):
        start = tile + (tile + 1) // 2
        extra = jnp.where((tile % 2 == 0) | (tile + 1 == hidden_tiles), 1, 0)
        lax.fori_loop(start, start + 1 + extra, lambda index, inner: (tick(index, "low"), inner)[1], 0)

        parity = tile % 2
        for copy in tile_copies(tile, parity):
            copy.wait()

        @pl.when(tile + 1 < hidden_tiles)
        def _():
            for copy in tile_copies(tile + 1, 1 - parity):
                copy.start()

        @pl.when(tile == 0)
        def _():
            for copy in wide_loads + out_loads:
                copy.start()

        @pl.when(tile >= 2)
        def _():
            du_store(tile - 2, parity).wait()

        u_cols = aligned(parity * SPAN, SPAN)
        u_tile = left[0, :, u_cols].astype(jnp.float32)
        square = u_tile * u_tile
        bend = jnp.tanh(GELU_C * u_tile * (1.0 + GELU_A * square))
        slope = 0.5 * (1.0 + bend) + (0.5 * GELU_C) * u_tile * (1.0 - bend * bend) * (
            1.0 + 3.0 * GELU_A * square
        )
        du_tile = (contract_last(dz_v[...], own_part[parity]) * slope).astype(jnp.bfloat16)
        kv_b[0, :, u_cols] = du_tile
        du_store(tile, parity).start()
        fresh = contract_last(du_tile, turned[0, aligned(parity * D, D), :])

        @pl.when(tile == 0)
        def _():
            dq_acc[...] = fresh

        @pl.when(tile > 0)
        def _():
            dq_acc[...] = dq_acc[...] + fresh

        return carry

    lax.fori_loop(0, hidden_tiles, ff_tile, 0)
    for tile in range(hidden_tiles - 2, hidden_tiles):
        du_store(tile, tile % 2).wait()
    for copy in wide_loads:
        copy.wait()
    for copy in block_copies(1):
        copy.start()

    def hidden_back(step, carry):
        gain1, gain2, bias1, bias2 = carry
        rows = aligned(step * CHAIN, CHAIN)
        upstream = dq_acc[rows, :]
        hat = hat2_v[rows, :].astype(jnp.float32)
        grad_h = dy_v[rows, :].astype(jnp.float32) + row_back(
            upstream, hat, lse_v[1, rows, 0:1], gain_ref[2:3, :]
        )
        gain2, bias2 = gain2 + column_sum(upstream * hat), bias2 + column_sum(upstream)
        dq_acc[rows, :] = grad_h
        if shallow:
            gkv[rows, :] = grad_h
        hat = hat1_v[rows, :].astype(jnp.float32)
        datt_v[rows, :] = row_back(grad_h, hat, lse_v[0, rows, 0:1], gain_ref[1:2, :]).astype(
            jnp.bfloat16
        )
        return gain1 + column_sum(grad_h * hat), gain2, bias1 + column_sum(grad_h), bias2

    zero = jnp.zeros((1, D), jnp.float32)
    sums = lax.fori_loop(0, BLK // CHAIN, hidden_back, (zero,) * 4)
    row = lax.broadcasted_iota(jnp.int32, (8, D), 0)
    norm_v[...] = norm_ref[...]
    for place, value in zip((1, 2, 5, 6), sums):
        norm_v[...] = norm_v[...] + jnp.where(row == place, value, 0.0)
    stores = [
        pltpu.make_async_copy(dq_acc, dh_hbm, sem_res.at[0]),
        pltpu.make_async_copy(datt_v, datt_hbm, sem_res.at[1]),
    ]
    lse_load = pltpu.make_async_copy(lse_hbm, lse_v, sem_in.at[0])
    for copy in stores + [lse_load]:
        copy.start()
    for place in range(4):
        out_loads[place].wait()
        do_v[:, pl.ds(place * TILE, TILE)] = contract_last(
            datt_v[...], term[place // 2, place % 2, :, pl.ds(0, D)]
        ).astype(jnp.bfloat16)
    for copy in stores + [lse_load]:
        copy.wait()
    dq_acc[...] = jnp.zeros_like(dq_acc)

    def attend(kv_ref, turned_ref, own, visible, begin):
        def body(group, carry):
            if shallow:
                tick(begin + group, "low")
            for member in range(PAIRED):
                grad_block(
                    q_v, do_v, o_v, lse_v, kv_ref, dq_acc, turned_ref, group * PAIRED + member, own, visible
                )
            return carry

        lax.fori_loop(0, groups, body, 0)

    def first_sums(piece, normed, cols):
        gain_sum[:, cols] = gain_sum[:, cols] + column_sum(piece * normed.astype(jnp.float32))
        bias_sum[:, cols] = bias_sum[:, cols] + column_sum(piece)

    gain_sum[...] = jnp.zeros_like(gain_sum)
    bias_sum[...] = jnp.zeros_like(bias_sum)

    def each_slot(slot, carry):
        visible = slot < own_slot
        index = slot + 1
        place = lax.rem(index, kv_b.shape[0])
        for copy in block_copies(index):
            copy.wait()
        if kv_b.shape[0] > 1:
            for copy in block_copies(index + 1):
                copy.start()
        begin = FF_TICKS + slot * block_ticks
        a_place = slot if shallow else 0
        attend(kv_b.at[place], turned.at[a_place], False, visible, begin)

        def weight_terms(step, inner):
            tick(begin + group_ticks + step, "low")
            rows = aligned(step * 512, 512)
            for part in range(0 if shallow else 2):
                cols = pl.ds(part * D, D)
                product = dot_dims(a_b[a_place, :, rows], turned[a_place, cols, :], 0, 1)
                for down in range(2):
                    target = term.at[step, down, :, pl.ds((part + 1) * D, D)]
                    piece = product[down * TILE : (down + 1) * TILE]

                    @pl.when(slot == 0)
                    def _(target=target, piece=piece):
                        target[...] = piece.astype(target.dtype)

                    @pl.when(slot > 0)
                    def _(target=target, piece=piece):
                        target[...] = (target[...] + piece).astype(target.dtype)

            piece = dot_dims(turned[a_place], weight[rows, pl.ds(D, 2 * D)], 0, 1)
            own_part[slot, :, rows] = piece.astype(jnp.bfloat16)
            first_sums(piece, a_b[a_place, :, rows], rows)
            return inner

        lax.fori_loop(0, 2, weight_terms, 0)
        if kv_b.shape[0] == 1:
            for copy in block_copies(index + 1):
                copy.start()
        return carry

    lax.fori_loop(0, slots, each_slot, 0)
    begin = FF_TICKS + slots * block_ticks
    own_place = (slots + 1) % kv_b.shape[0]
    for copy in block_copies(slots + 1):
        copy.wait()
    own_a = slots if shallow else 0
    attend(kv_b.at[own_place], turned.at[own_a], True, None, begin)
    dq_low[...] = (dq_acc[...] * ALPHA).astype(jnp.bfloat16) * jnp.bfloat16(QSCALE)
    x_load = pltpu.make_async_copy(x_hbm, do_v, sem_in.at[0])
    x_load.start()
    ready = begin + group_ticks

    def last_terms(step, carry):
        tick(begin + group_ticks + step, "both")
        rows = aligned(step * TILE, TILE)
        a_rows = a_b[0, :, rows]
        up, down = step // 2, step % 2
        term[up, down, :, pl.ds(0, D)] = dot_dims(a_rows, dq_low[...], 0, 0).astype(jnp.bfloat16)
        for part in range(2):
            cols = pl.ds(part * D, D)
            target = term.at[up, down, :, pl.ds((part + 1) * D, D)]
            target[...] = (target[...] + dot_dims(a_rows, turned[0, cols, :], 0, 1)).astype(jnp.bfloat16)
        return carry

    if not shallow:
        lax.fori_loop(0, 4, last_terms, 0)
        ready = ready + 4
    assert ready <= last_low - 2
    da_acc = dq_acc

    spare = max(0, last_low - 2 - ready - 4) if shallow else 0

    def own_grad(step, carry):
        if shallow:
            begins = ready + step + jnp.where(step > 0, spare, 0)
            ends = ready + step + 1 + spare
            lax.fori_loop(begins, ends, lambda index, inner: (tick(index, "low"), inner)[1], 0)
        else:
            tick(ready + step, "low")
        rows = aligned(step * TILE, TILE)
        piece = dot_dims(dq_low[...], weight[rows, pl.ds(0, D)], 1, 1) + dot_dims(
            turned[own_a], weight[rows, pl.ds(D, 2 * D)], 0, 1
        )
        da_acc[:, rows] = piece
        first_sums(piece, a_b[own_a, :, rows], rows)
        return carry

    lax.fori_loop(0, 4, own_grad, 0)
    ready = ready + 4 + spare

    first_gain = (gain_sum[...] - bias_ref[0:1, :] * bias_sum[...]) / gain_ref[0:1, :]
    norm_v[...] = (
        norm_v[...] + jnp.where(row == 0, first_gain, 0.0) + jnp.where(row == 4, bias_sum[...], 0.0)
    )

    def run_ticks(first, last, kinds):
        if last > first:
            lax.fori_loop(first, last, lambda index, carry: (tick(index, kinds), carry)[1], 0)
        return max(first, last)

    assert ready == last_low - 2 or not shallow
    norm_peers = [core_peer, side_peer, grp_peer] + level_peers
    norm_base = ready
    norm_result = pltpu.make_async_copy(norm_v, norm_out, sem_res.at[1])

    def norm_move(place):
        return remote(norm_v, norm_in.at[place], norm_s.at[place], norm_r.at[place], norm_peers[place])

    def norm_ticks(step, carry):
        for place in range(len(norm_peers) + 1):

            @pl.when(step == norm_base + 3 * place)
            def _(place=place):
                if place:
                    finished(norm_move(place - 1))
                    norm_v[...] = norm_v[...] + norm_in[place - 1]
                if place < len(norm_peers):
                    norm_move(place).start()
                else:
                    norm_result.start()

        tick(step, "high")
        return carry

    last_tick = max(ready + 3 * len(norm_peers) + 1, chain_ticks)
    lax.fori_loop(ready, last_tick, norm_ticks, 0)
    ready = last_tick
    x_load.wait()
    gain = gain_ref[0:1, :]

    def norm_grad(step, carry):
        @pl.when(step % 2 == 0)
        def _():
            tick(ready + step // 2, "none")

        rows = aligned(step * CHAIN, CHAIN)
        upstream = da_acc[rows, :]
        for slot in range(slots):
            joined = left[slot, rows, :].astype(jnp.float32) + right[slot, rows, :].astype(jnp.float32)
            upstream = upstream + jnp.where(own_slot == slot, joined, 0.0)
        values = do_v[rows, :].astype(jnp.float32)
        centre = values - jnp.mean(values, axis=-1, keepdims=True)
        scale = lax.rsqrt(jnp.mean(centre * centre, axis=-1, keepdims=True) + EPS)
        centre = centre * scale
        grad = row_back(upstream, centre, scale, gain)
        da_acc[rows, :] = grad + gkv[rows, :] if shallow else grad
        return carry

    lax.fori_loop(0, BLK // CHAIN, norm_grad, 0)
    ready = ready + BLK // CHAIN // 2
    result = pltpu.make_async_copy(da_acc, grad_out, sem_res.at[0])
    result.start()
    run_ticks(ready, all_ticks, "none")

    def drain_chain(index, carry):
        here = left.at[0, pl.ds(0, CHAIN)]

        @pl.when(ctx < n_ctx - 1)
        def _():
            remote(here, here, left_s.at[index], left_r.at[index], next_ctx).wait_send()

        @pl.when(ctx > 0)
        def _():
            remote(here, here, right_s.at[index], right_r.at[index], last_ctx).wait_send()

        return carry

    lax.fori_loop(0, chain_chunks, drain_chain, 0)
    result.wait()
    norm_result.wait()


def backward_part(n_ctx, slot_vec, gains, biases, norms, saved, weights, ffn):
    slots = n_ctx // 2
    levels = n_ctx.bit_length() - 1
    depth = 16 if n_ctx == 4 else 10
    hidden = weights[1].shape[1]
    widths = [(hidden // 4, D), (D // 4, hidden), (D // 4, D), (D // 4, 3 * D)]
    low, full = jnp.bfloat16, jnp.float32
    dma = pltpu.SemaphoreType.DMA
    hbm = pl.BlockSpec(memory_space=pl.ANY)
    vmem = pl.BlockSpec(memory_space=pltpu.VMEM)
    shape = jax.ShapeDtypeStruct
    buffers = 2 if slots <= 2 else 1
    chain = slots * (BLK // CHAIN)
    zshapes, rows, cols = [], TILE // 2, TILE
    if n_ctx == 4:
        zshapes = [pltpu.VMEM((depth, rows, cols), low), pltpu.VMEM((depth, rows // 2, cols), low)]
    for _ in range(0 if zshapes else levels):
        rows, cols = (rows // 2, cols) if rows > 16 else (rows, cols // 2)
        zshapes.append(pltpu.VMEM((depth, rows, cols), low))
    return pl.pallas_call(
        functools.partial(backward_kernel, n_ctx, widths),
        out_shape=[shape(width, low) for width in widths] + [
            shape((BLK, D), full),
            shape((8, D), full),
            shape((BLK, D), full),
            shape((BLK, hidden), low),
            shape((BLK, D), low),
        ],
        in_specs=[pl.BlockSpec(memory_space=pltpu.SMEM), vmem, vmem, vmem]
        + [hbm] * (len(saved) + len(weights) + len(ffn)),
        out_specs=[hbm] * 9,
        scratch_shapes=[
            pltpu.VMEM((BLK, D), low),
            pltpu.VMEM((BLK, D), low),
            pltpu.VMEM((BLK, D), low),
            pltpu.VMEM((PAIRS, BLK, 128), full),
            pltpu.VMEM((D, 3 * D), low),
            pltpu.VMEM((buffers, BLK, 2 * D), low),
            pltpu.VMEM((slots + 1 if slots <= 2 else 1, BLK, D), low),
            pltpu.VMEM((BLK, D), full),
            pltpu.VMEM((slots + 1 if slots <= 2 else 1, 2 * D, BLK), low),
            pltpu.VMEM((BLK, D) if slots <= 2 else (8, 128), full),
            pltpu.VMEM((2, 2, D // 4, D if slots <= 2 else 3 * D), low),
            pltpu.VMEM((slots, BLK, D), low),
            pltpu.VMEM((slots, BLK, D), low),
            pltpu.VMEM((slots, BLK, D), low),
            pltpu.VMEM((8, D), full),
            pltpu.VMEM((3 + levels, 8, D), full),
            pltpu.VMEM((1, D), full),
            pltpu.VMEM((1, D), full),
            pltpu.VMEM((depth, 2, TILE, TILE), low),
            pltpu.VMEM((depth, TILE, TILE), low),
            pltpu.VMEM((depth, TILE // 2, TILE), low),
            pltpu.VMEM((depth, TILE, TILE), low),
            pltpu.VMEM((4, 2, 2, TILE, TILE), low),
        ]
        + [pltpu.VMEM((2, 4, BLK, TILE), low), pltpu.VMEM((4, BLK, TILE), low)]
        + zshapes
        + [dma((12,)), dma((2, buffers)), dma((4,)), dma((2, 4)), dma((4, 2)), dma((depth,)), dma((2,))]
        + [dma((depth,))] * (8 + 4 * levels)
        + [dma((chain,))] * 4
        + [dma((3 + levels,))] * 2,
        compiler_params=pltpu.CompilerParams(
            collective_id=2, has_side_effects=True, vmem_limit_bytes=67043328
        ),
        cost_estimate=pl.CostEstimate(flops=40 << 30, bytes_accessed=64 << 20, transcendentals=1 << 24),
        name="attend_back_reduce",
    )(
        slot_vec,
        gains,
        biases,
        norms,
        *saved,
        *weights,
        *ffn,
    )


def widen_kernel(*refs):
    count = len(refs) // 2
    for source, dest in zip(refs[: count - 1], refs[count:]):
        dest[...] = source[...].astype(dest.dtype)
    refs[-2][...] = refs[count - 1][0:4, :]
    refs[-1][...] = refs[count - 1][4:8, :]


def widen(arrays, types, norms):
    steps = 8
    specs = [pl.BlockSpec((x.shape[0] // steps, x.shape[1]), lambda i: (i, 0)) for x in arrays]
    shape = jax.ShapeDtypeStruct
    pair = [pl.BlockSpec((4, D), lambda i: (0, 0))] * 2
    return pl.pallas_call(
        widen_kernel,
        out_shape=[shape(x.shape, kind) for x, kind in zip(arrays, types)]
        + [shape((4, D), jnp.float32)] * 2,
        grid=(steps,),
        in_specs=specs + [pl.BlockSpec((8, D), lambda i: (0, 0))],
        out_specs=specs + pair,
        compiler_params=pltpu.CompilerParams(vmem_limit_bytes=67043328),
        name="widen",
    )(*arrays, norms)


def per_device(n_ctx, inputs, w_qkv, w_out, w_up, w_down, norm_gains, norm_biases, block_map, out_grad):
    slots = n_ctx // 2
    raw, seed_low = inputs.reshape(BLK, D), out_grad.reshape(BLK, D)
    block_entry = block_map.reshape(2)
    forward = forward_part(
        n_ctx,
        block_entry,
        norm_gains,
        norm_biases,
        raw,
        seed_low,
        w_qkv,
        w_out,
        w_up,
        w_down,
    )
    every_low, queries, keys_values, attn_low, lse, full_qkv, full_out, full_up, full_down = forward[:9]
    result, active_low, down_low, ffn_low, upward, hat1, hat2, rstd, norms = forward[9:]
    backward = backward_part(
        n_ctx,
        block_entry,
        norm_gains,
        norm_biases,
        norms,
        [raw, queries, keys_values, every_low, attn_low, lse, full_qkv],
        [full_out, full_up, full_down],
        [active_low, down_low, ffn_low, upward, hat1, hat2, rstd, seed_low],
    )
    grad_tokens, norm_total, grad_hidden = backward[4:7]
    if slots > 2:
        grad_tokens = grad_tokens + grad_hidden
    full = jnp.float32
    summed_down, summed_up, summed_out, summed_qkv, grad_input, result, gain_total, bias_total = widen(
        list(backward[:4]) + [grad_tokens, result],
        [full] * 5 + [jnp.bfloat16],
        norm_total,
    )
    return (
        result.reshape(1, 1, BLK, D),
        grad_input.reshape(1, 1, BLK, D),
        summed_qkv,
        summed_out,
        summed_up,
        summed_down,
        gain_total,
        bias_total,
    )


def solution(mesh):
    rows = P("wsh", None)
    blocks = P("grp", "wsh", "ctx", None)
    return jax.shard_map(
        functools.partial(per_device, mesh.shape["ctx"]),
        mesh=mesh,
        in_specs=(blocks, rows, rows, rows, rows, P(), P(), blocks, blocks),
        out_specs=(blocks, blocks, rows, rows, rows, rows, P(), P()),
        check_vma=False,
    )
```

profile of v0, /device:TPU:0, one launch (start us, length us, event | category | flops | bytes accessed | tf_op | source)
XLA Modules:
  0.0 327.0 jit_solution(10971680384041254633)
XLA Ops:
  0.6 128.2 %gather_attend.1 = (bf16[1536,1024]{1,0:T(8,128)(2,1)}, bf16[512,1024]{1,0:T(8,128)(2,1)}, bf16[1536,2048]{1,0:T(8,128)(2,1)}, bf16[512,1024]{1,0:T(8,128)(2,1)}...) custom-call(s32[2]{0:T(128)} %bitcast.11, ...), custom_call_target="tpu_custom_call" | custom-call | flops 21474836480 | bytes 67108864 | tf_op jit(solution)/shard_map/gather_attend/pallas_call | solution.py:678
  128.8 187.3 %attend_back_reduce.1 = (bf16[1024,1024]{1,0:T(8,128)(2,1)}, bf16[256,4096]{1,0:T(8,128)(2,1)}, bf16[256,1024]{1,0:T(8,128)(2,1)}, bf16[256,3072]{1,0:T(8,128)(2...) custom-call(s32[2]{0:T(128)} %bitcast.12, ...), custom_call_target="tpu_custom_call" | custom-call | flops 42949672960 | bytes 67108864 | tf_op jit(solution)/shard_map/attend_back_reduce/pallas_call | solution.py:1573
  316.1 10.6 %widen.1 = (f32[1024,1024]{1,0:T(8,128)}, f32[256,4096]{1,0:T(8,128)}, f32[256,1024]{1,0:T(8,128)}, f32[256,3072]{1,0:T(8,128)}, f32[512,1024]{1,0:T(8,128)}, /*...) custom-call(bf16[1024,1024]{1,0:T(8,128)(2,1)} %get-tuple-element.57.refs_0_, ...), custom_call_target="tpu_custom_call" | custom-call | tf_op jit(solution)/shard_map/widen/pallas_call | solution.py:1645
where the time goes:
time: 328 us; the launch traced here: 327 us
  Pallas kernels  326 us (99%)
    pallas_call x1, Pallas kernels, backward_part(): pl.pallas_call(functools.partial(backward_kernel, n_ctx, widths), out_sha...  187 us
    pallas_call x1, Pallas kernels, forward_part(): pl.pallas_call(functools.partial(forward_kernel, n_ctx), out_shape=[shape...  128 us
    pallas_call x1, Pallas kernels, widen(): pl.pallas_call(widen_kernel, out_shape=[shape(x.shape, kind) for x, kind...  10.6 us

commit v1 on v0

--- a/solution.py
+++ b/solution.py
@@ -529,13 +529,17 @@
         copy.wait()
     shallow_tiles = full_up.shape[1] // SPAN
 
-    def tile_loads(tile, parity):
+    def down_spot(place):
+        return aligned(BLK + (place // 2) * BLK, BLK), aligned((place % 2) * D, D)
+
+    def tile_loads(tile, place):
         cols = aligned(tile * SPAN, SPAN)
+        spot = down_spot(place)
         return (
             pltpu.make_async_copy(
-                full_up.at[:, cols], weight.at[:, aligned(D + parity * SPAN, SPAN)], sem_ff.at[0, parity]
+                full_up.at[:, cols], weight.at[:, aligned(D + place * SPAN, SPAN)], sem_ff.at[0, place]
             ),
-            pltpu.make_async_copy(full_down.at[cols, :], left.at[parity], sem_ff.at[1, parity]),
+            pltpu.make_async_copy(full_down.at[cols, :], kv_all.at[spot[0], spot[1]], sem_ff.at[1, place]),
         )
 
     def tile_stores(tile, parity):
@@ -551,7 +555,7 @@
 
     out_load = pltpu.make_async_copy(full_out, weight.at[:, pl.ds(0, D)], sem_in.at[0])
     x_load = pltpu.make_async_copy(x_hbm, right.at[1], sem_in.at[1])
-    for copy in (out_load, x_load) + tile_loads(0, 0):
+    for copy in (out_load, x_load):
         copy.start()
 
     def drain_blocks(index, carry):
@@ -561,6 +565,9 @@
         return carry
 
     lax.fori_loop(0, slots + 1, drain_blocks, 0)
+    for tile in range(3):
+        for copy in tile_loads(tile, tile):
+            copy.start()
     out_load.wait()
     for half_cols in range(2):
         cols = pl.ds(half_cols * SPAN, SPAN)
@@ -595,13 +602,13 @@
         copy.start()
 
     def ff_tile(tile, carry):
-        parity = tile % 2
-        for copy in tile_loads(tile, parity):
+        parity, place = tile % 2, tile % 4
+        for copy in tile_loads(tile, place):
             copy.wait()
 
-        @pl.when(tile + 1 < shallow_tiles)
-        def _():
-            for copy in tile_loads(tile + 1, 1 - parity):
+        @pl.when(tile + 3 < shallow_tiles)
+        def _():
+            for copy in tile_loads(tile + 3, (tile + 3) % 4):
                 copy.start()
 
         @pl.when(tile >= 2)
@@ -610,7 +617,7 @@
                 copy.wait()
 
         upward = jnp.dot(
-            q_all[...], weight[:, aligned(D + parity * SPAN, SPAN)], preferred_element_type=jnp.float32
+            q_all[...], weight[:, aligned(D + place * SPAN, SPAN)], preferred_element_type=jnp.float32
         )
         kv_all[pl.ds(0, BLK), aligned(parity * SPAN, SPAN)] = upward.astype(jnp.bfloat16)
         active = (
@@ -619,7 +626,8 @@
         kv_all[pl.ds(0, BLK), aligned(D + parity * SPAN, SPAN)] = active
         for copy in tile_stores(tile, parity):
             copy.start()
-        fresh = jnp.dot(active, left[parity], preferred_element_type=jnp.float32)
+        spot = down_spot(place)
+        fresh = jnp.dot(active, kv_all[spot[0], spot[1]], preferred_element_type=jnp.float32)
 
         @pl.when(tile == 0)
         def _():
@@ -715,7 +723,7 @@
             dma((3,)),
             dma((3,)),
             dma((3,)),
-            dma((4, 2)),
+            dma((4, 4)),
             dma((4,)),
             dma((slots + 1,)),
             dma((slots + 1,)),
@@ -921,10 +929,15 @@
                             copy.start()
 
             right_side = rhs[near]
-            for owner in range(4):
-                made[near, owner // 2, owner % 2] = dot_dims(
-                    lhs[parity, owner], right_side, 0, 0
-                ).astype(jnp.bfloat16)
+
+            def owner_pair(upper, carry):
+                for core_of in range(2):
+                    made[near, upper, core_of] = dot_dims(
+                        lhs[parity, upper * 2 + core_of], right_side, 0, 0
+                    ).astype(jnp.bfloat16)
+                return carry
+
+            lax.fori_loop(0, 2, owner_pair, 0)
 
         def high_piece():
             number = index - last_low
@@ -1638,7 +1651,7 @@
 
 
 def widen(arrays, types, norms):
-    steps = 8
+    steps = 4
     specs = [pl.BlockSpec((x.shape[0] // steps, x.shape[1]), lambda i: (i, 0)) for x in arrays]
     shape = jax.ShapeDtypeStruct
     pair = [pl.BlockSpec((4, D), lambda i: (0, 0))] * 2

time: 328 us -> 331 us (level)
  Pallas kernels: 326 us -> 330 us
where the time goes in v1:
time: 331 us; the launch traced here: 330 us
  Pallas kernels  330 us (100%)
    pallas_call x1, Pallas kernels, backward_part(): pl.pallas_call(functools.partial(backward_kernel, n_ctx, widths), out_sha...  190 us
    pallas_call x1, Pallas kernels, forward_part(): pl.pallas_call(functools.partial(forward_kernel, n_ctx), out_shape=[shape...  129 us
    pallas_call x1, Pallas kernels, widen(): pl.pallas_call(widen_kernel, out_shape=[shape(x.shape, kind) for x, kind...  10.2 us

profile of v1, /device:TPU:0, one launch (start us, length us, event | category | flops | bytes accessed | tf_op | source)
XLA Modules:
  0.0 330.4 jit_solution(5298355294566116544)
XLA Ops:
  0.6 129.1 %gather_attend.1 = (bf16[1536,1024]{1,0:T(8,128)(2,1)}, bf16[512,1024]{1,0:T(8,128)(2,1)}, bf16[1536,2048]{1,0:T(8,128)(2,1)}, bf16[512,1024]{1,0:T(8,128)(2,1)}...) custom-call(s32[2]{0:T(128)} %bitcast.11, ...), custom_call_target="tpu_custom_call" | custom-call | flops 21474836480 | bytes 67108864 | tf_op jit(solution)/shard_map/gather_attend/pallas_call | solution.py:686
  129.7 190.3 %attend_back_reduce.1 = (bf16[1024,1024]{1,0:T(8,128)(2,1)}, bf16[256,4096]{1,0:T(8,128)(2,1)}, bf16[256,1024]{1,0:T(8,128)(2,1)}, bf16[256,3072]{1,0:T(8,128)(2...) custom-call(s32[2]{0:T(128)} %bitcast.12, ...), custom_call_target="tpu_custom_call" | custom-call | flops 42949672960 | bytes 67108864 | tf_op jit(solution)/shard_map/attend_back_reduce/pallas_call | solution.py:1586
  320.0 10.2 %widen.1 = (f32[1024,1024]{1,0:T(8,128)}, f32[256,4096]{1,0:T(8,128)}, f32[256,1024]{1,0:T(8,128)}, f32[256,3072]{1,0:T(8,128)}, f32[512,1024]{1,0:T(8,128)}, /*...) custom-call(bf16[1024,1024]{1,0:T(8,128)(2,1)} %get-tuple-element.57.refs_0_, ...), custom_call_target="tpu_custom_call" | custom-call | tf_op jit(solution)/shard_map/widen/pallas_call | solution.py:1658

commit v2 on v0

--- a/solution.py
+++ b/solution.py
@@ -838,7 +838,6 @@
     peers = [core_peer, side_peer, grp_peer, next_ctx, last_ctx] + level_peers
     for peer in peers:
         pl.semaphore_signal(barrier, inc=1, device_id=peer, device_id_type=MESH)
-    pl.semaphore_wait(barrier, len(peers))
 
     half = TILE // 2
     ranges, first = [], 0
@@ -1262,6 +1261,7 @@
         )
         for place in range(4)
     ]
+    pl.semaphore_wait(barrier, len(peers))
     lax.fori_loop(0, 2, lambda index, carry: (step_make(index, "low"), carry)[1], 0)
     dz_load.wait()
 
@@ -1638,7 +1638,7 @@
 
 
 def widen(arrays, types, norms):
-    steps = 8
+    steps = 4
     specs = [pl.BlockSpec((x.shape[0] // steps, x.shape[1]), lambda i: (i, 0)) for x in arrays]
     shape = jax.ShapeDtypeStruct
     pair = [pl.BlockSpec((4, D), lambda i: (0, 0))] * 2

time: 328 us -> 330 us (level); the launches traced: 327 us -> 325 us
  no operation moved by 1% of the time
where the time goes in v2:
time: 330 us; the launch traced here: 325 us
  Pallas kernels  324 us (98%)
    pallas_call x1, Pallas kernels, backward_part(): pl.pallas_call(functools.partial(backward_kernel, n_ctx, widths), out_sha...  186 us
    pallas_call x1, Pallas kernels, forward_part(): pl.pallas_call(functools.partial(forward_kernel, n_ctx), out_shape=[shape...  128 us
    pallas_call x1, Pallas kernels, widen(): pl.pallas_call(widen_kernel, out_shape=[shape(x.shape, kind) for x, kind...  10.2 us

profile of v2, /device:TPU:0, one launch (start us, length us, event | category | flops | bytes accessed | tf_op | source)
XLA Modules:
  0.0 325.1 jit_solution(8578941905830068113)
XLA Ops:
  0.6 128.2 %gather_attend.1 = (bf16[1536,1024]{1,0:T(8,128)(2,1)}, bf16[512,1024]{1,0:T(8,128)(2,1)}, bf16[1536,2048]{1,0:T(8,128)(2,1)}, bf16[512,1024]{1,0:T(8,128)(2,1)}...) custom-call(s32[2]{0:T(128)} %bitcast.11, ...), custom_call_target="tpu_custom_call" | custom-call | flops 21474836480 | bytes 67108864 | tf_op jit(solution)/shard_map/gather_attend/pallas_call | solution.py:678
  128.8 185.8 %attend_back_reduce.1 = (bf16[1024,1024]{1,0:T(8,128)(2,1)}, bf16[256,4096]{1,0:T(8,128)(2,1)}, bf16[256,1024]{1,0:T(8,128)(2,1)}, bf16[256,3072]{1,0:T(8,128)(2...) custom-call(s32[2]{0:T(128)} %bitcast.12, ...), custom_call_target="tpu_custom_call" | custom-call | flops 42949672960 | bytes 67108864 | tf_op jit(solution)/shard_map/attend_back_reduce/pallas_call | solution.py:1573
  314.7 10.2 %widen.1 = (f32[1024,1024]{1,0:T(8,128)}, f32[256,4096]{1,0:T(8,128)}, f32[256,1024]{1,0:T(8,128)}, f32[256,3072]{1,0:T(8,128)}, f32[512,1024]{1,0:T(8,128)}, /*...) custom-call(bf16[1024,1024]{1,0:T(8,128)(2,1)} %get-tuple-element.57.refs_0_, ...), custom_call_target="tpu_custom_call" | custom-call | tf_op jit(solution)/shard_map/widen/pallas_call | solution.py:1645

commit v3 on v2

--- a/solution.py
+++ b/solution.py
@@ -562,9 +562,13 @@
 
     lax.fori_loop(0, slots + 1, drain_blocks, 0)
     out_load.wait()
-    for half_cols in range(2):
-        cols = pl.ds(half_cols * SPAN, SPAN)
+
+    def out_half(index, carry):
+        cols = aligned(index * SPAN, SPAN)
         acc[:, cols] = jnp.dot(x_own[...], weight[:, cols], preferred_element_type=jnp.float32)
+        return carry
+
+    lax.fori_loop(0, D // SPAN, out_half, 0)
     x_load.wait()
     for copy in outputs[2:]:
         copy.wait()
@@ -1349,11 +1353,16 @@
     lse_load = pltpu.make_async_copy(lse_hbm, lse_v, sem_in.at[0])
     for copy in stores + [lse_load]:
         copy.start()
-    for place in range(4):
-        out_loads[place].wait()
-        do_v[:, pl.ds(place * TILE, TILE)] = contract_last(
+    for load in out_loads:
+        load.wait()
+
+    def out_back(place, carry):
+        do_v[:, aligned(place * TILE, TILE)] = contract_last(
             datt_v[...], term[place // 2, place % 2, :, pl.ds(0, D)]
         ).astype(jnp.bfloat16)
+        return carry
+
+    lax.fori_loop(0, 4, out_back, 0)
     for copy in stores + [lse_load]:
         copy.wait()
     dq_acc[...] = jnp.zeros_like(dq_acc)

time: 330 us -> 326 us (0.988); the launches traced: 325 us -> 325 us
  no operation moved by 1% of the time
where the time goes in v3:
time: 326 us; the launch traced here: 325 us
  Pallas kernels  324 us (99%)
    pallas_call x1, Pallas kernels, backward_part(): pl.pallas_call(functools.partial(backward_kernel, n_ctx, widths), out_sha...  186 us
    pallas_call x1, Pallas kernels, forward_part(): pl.pallas_call(functools.partial(forward_kernel, n_ctx), out_shape=[shape...  128 us
    pallas_call x1, Pallas kernels, widen(): pl.pallas_call(widen_kernel, out_shape=[shape(x.shape, kind) for x, kind...  10.2 us

profile of v3, /device:TPU:0, one launch (start us, length us, event | category | flops | bytes accessed | tf_op | source)
XLA Modules:
  0.0 325.3 jit_solution(11657609299657201564)
XLA Ops:
  0.6 128.4 %gather_attend.1 = (bf16[1536,1024]{1,0:T(8,128)(2,1)}, bf16[512,1024]{1,0:T(8,128)(2,1)}, bf16[1536,2048]{1,0:T(8,128)(2,1)}, bf16[512,1024]{1,0:T(8,128)(2,1)}...) custom-call(s32[2]{0:T(128)} %bitcast.11, ...), custom_call_target="tpu_custom_call" | custom-call | flops 21474836480 | bytes 67108864 | tf_op jit(solution)/shard_map/gather_attend/pallas_call | solution.py:682
  129.0 185.9 %attend_back_reduce.1 = (bf16[1024,1024]{1,0:T(8,128)(2,1)}, bf16[256,4096]{1,0:T(8,128)(2,1)}, bf16[256,1024]{1,0:T(8,128)(2,1)}, bf16[256,3072]{1,0:T(8,128)(2...) custom-call(s32[2]{0:T(128)} %bitcast.12, ...), custom_call_target="tpu_custom_call" | custom-call | flops 42949672960 | bytes 67108864 | tf_op jit(solution)/shard_map/attend_back_reduce/pallas_call | solution.py:1582
  314.9 10.2 %widen.1 = (f32[1024,1024]{1,0:T(8,128)}, f32[256,4096]{1,0:T(8,128)}, f32[256,1024]{1,0:T(8,128)}, f32[256,3072]{1,0:T(8,128)}, f32[512,1024]{1,0:T(8,128)}, /*...) custom-call(bf16[1024,1024]{1,0:T(8,128)(2,1)} %get-tuple-element.57.refs_0_, ...), custom_call_target="tpu_custom_call" | custom-call | tf_op jit(solution)/shard_map/widen/pallas_call | solution.py:1654

commit v4 on v3

--- a/solution.py
+++ b/solution.py
@@ -1283,7 +1283,7 @@
             for copy in tile_copies(tile + 1, 1 - parity):
                 copy.start()
 
-        @pl.when(tile == 0)
+        @pl.when(tile == 2)
         def _():
             for copy in wide_loads + out_loads:
                 copy.start()

time: 326 us -> 326 us (level)
  no operation moved by 1% of the time
where the time goes in v4:
time: 326 us; the launch traced here: 325 us
  Pallas kernels  325 us (100%)
    pallas_call x1, Pallas kernels, backward_part(): pl.pallas_call(functools.partial(backward_kernel, n_ctx, widths), out_sha...  186 us
    pallas_call x1, Pallas kernels, forward_part(): pl.pallas_call(functools.partial(forward_kernel, n_ctx), out_shape=[shape...  128 us
    pallas_call x1, Pallas kernels, widen(): pl.pallas_call(widen_kernel, out_shape=[shape(x.shape, kind) for x, kind...  10.2 us

profile of v4, /device:TPU:0, one launch (start us, length us, event | category | flops | bytes accessed | tf_op | source)
XLA Modules:
  0.0 325.4 jit_solution(8017141930456664638)
XLA Ops:
  0.6 128.4 %gather_attend.1 = (bf16[1536,1024]{1,0:T(8,128)(2,1)}, bf16[512,1024]{1,0:T(8,128)(2,1)}, bf16[1536,2048]{1,0:T(8,128)(2,1)}, bf16[512,1024]{1,0:T(8,128)(2,1)}...) custom-call(s32[2]{0:T(128)} %bitcast.11, ...), custom_call_target="tpu_custom_call" | custom-call | flops 21474836480 | bytes 67108864 | tf_op jit(solution)/shard_map/gather_attend/pallas_call | solution.py:682
  129.0 186.0 %attend_back_reduce.1 = (bf16[1024,1024]{1,0:T(8,128)(2,1)}, bf16[256,4096]{1,0:T(8,128)(2,1)}, bf16[256,1024]{1,0:T(8,128)(2,1)}, bf16[256,3072]{1,0:T(8,128)(2...) custom-call(s32[2]{0:T(128)} %bitcast.12, ...), custom_call_target="tpu_custom_call" | custom-call | flops 42949672960 | bytes 67108864 | tf_op jit(solution)/shard_map/attend_back_reduce/pallas_call | solution.py:1582
  315.0 10.2 %widen.1 = (f32[1024,1024]{1,0:T(8,128)}, f32[256,4096]{1,0:T(8,128)}, f32[256,1024]{1,0:T(8,128)}, f32[256,3072]{1,0:T(8,128)}, f32[512,1024]{1,0:T(8,128)}, /*...) custom-call(bf16[1024,1024]{1,0:T(8,128)(2,1)} %get-tuple-element.57.refs_0_, ...), custom_call_target="tpu_custom_call" | custom-call | tf_op jit(solution)/shard_map/widen/pallas_call | solution.py:1654
